TPU v7x, 32 devices: a whole 2x2x4 slice. The times are simulated.
32 devices in a mesh: frame: 4 (over y, x), head: 8 (over z, core).
Axes of the slice: x: 2, y: 2, z: 4, core: 2. Of those that a mesh axis runs over, the one named last changes fastest.
Arguments:
- tokens: float32 [8, 1024, 1024], P('frame', 'head'), may hold values from -48 to 48
- qkv_weight: float32 [1024, 3072], replicated
- out_weight: float32 [1024, 1024], replicated, may hold values from -0.1875 to 0.1875
- norm_gain: float32 [1024], replicated, may hold values from 0.1 to 1.9
- proj_weight: float32 [1024, 256], replicated, may hold values from -0.1875 to 0.1875
- up_weight: bfloat16 [256, 4096], replicated, may hold values from -0.375 to 0.375
- conv_weight: bfloat16 [2, 3, 3, 256, 256], replicated, may hold values from -0.125 to 0.125
- conv_bias: float32 [2, 256], replicated, may hold values from -3 to 3
- block_lists: int32 [64, 13], P('frame'), may hold values from 0 to 63, as said below
- block_counts: int32 [64], P('frame'), may hold values from 1 to 13, as said below
Outputs:
- refined: bfloat16 [8, 128, 128, 256], P('frame', 'head')
Inputs may be any that keep to these rules, and one draw needn't show every extreme that they name: `block_lists`: row b names 13 different key blocks and its first entry is block b itself; entries at or after the row's count are padding and are ignored. `block_counts`: some query block in every draw has all 13 entries valid.
All inputs are finite; a program needn't handle non-finite values.
Results may differ from a plain program's by a relative error of at most 0.0057.
Values may be sent and summed in bfloat16 or wider, within the bound.
A program may use at most 128 MiB of HBM per device.

v0:
```python
import math
import jax
import jax.numpy as jnp
from jax import lax
from jax.sharding import PartitionSpec as P

HEADS = 16
GRID = 32
BLOCK = 128
highest = lax.Precision.HIGHEST
eps_norm = 1e-05


def extended_2(block, sides, width):
    for axis, dim in sides:
        count = lax.axis_size(axis)
        forward = [(i, i + 1) for i in range(count - 1)]
        backward = [(target, source) for source, target in forward]
        low = lax.ppermute(
            lax.slice_in_dim(block, block.shape[dim] - width, None, axis=dim), axis, forward
        )
        high = lax.ppermute(lax.slice_in_dim(block, 0, width, axis=dim), axis, backward)
        block = jnp.concatenate([low, block, high], axis=dim)
    return block


def attend_padded(queries, key_values, block_ids, counts, factor):
    groups, slot_total = block_ids.shape
    block_size = queries.shape[1]
    half = queries.shape[3] // 2
    picked = key_values[block_ids]
    picked = picked.reshape((groups, slot_total * block_size) + picked.shape[3:])
    scores = jnp.einsum("gihe,gjhe->ghij", queries, picked, precision=highest) * factor
    slot_of = jnp.arange(slot_total * block_size, dtype=jnp.int32) // block_size
    usable = slot_of[None, :] < counts[:, None]
    scores = jnp.where(usable[:, None, None, :], scores, -jnp.inf)
    row_max = jnp.max(scores, axis=3, keepdims=True)
    weights = jnp.exp(scores - row_max)
    totals = jnp.sum(weights, axis=3)
    blended = jnp.einsum("ghij,gjhe->gihe", weights, picked, precision=highest)
    return blended[:, :, :, half:] / jnp.transpose(totals, (0, 2, 1))[:, :, :, None]


def layer_norm(rows, gain):
    centre = jnp.mean(rows, axis=-1, keepdims=True)
    centred = rows - centre
    spread = jnp.mean(centred * centred, axis=-1, keepdims=True)
    return centred * lax.rsqrt(spread + eps_norm) * gain


def conv_window(padded, weight):
    frames_here, rows_in, cols_in, channels = padded.shape
    rows_out = rows_in - 2
    cols_out = cols_in - 2
    summed = jnp.zeros((frames_here * rows_out * cols_out, weight.shape[-1]), jnp.float32)
    for row_off in range(3):
        for col_off in range(3):
            window = padded[:, row_off : row_off + rows_out, col_off : col_off + cols_out, :]
            summed = summed + jnp.dot(
                window.reshape(-1, channels),
                weight[row_off, col_off],
                preferred_element_type=jnp.float32,
            )
    return summed.reshape(frames_here, rows_out, cols_out, -1)


def pad_columns(image):
    return jnp.pad(image, ((0, 0), (0, 0), (1, 1), (0, 0)))


def on_device(
    tokens,
    qkv_weight,
    out_weight,
    norm_gain,
    proj_weight,
    up_weight,
    conv_weight,
    conv_bias,
    block_lists,
    block_counts,
):
    local_frames, strip_tokens, model_width = tokens.shape
    head_groups = lax.axis_size("head")
    local_heads = HEADS // head_groups
    head_dim = model_width // HEADS
    column_width = local_heads * 3 * head_dim
    frame_tokens = strip_tokens * head_groups
    flat_strip = tokens.reshape(-1, model_width)
    columns = lax.dynamic_slice_in_dim(
        qkv_weight, lax.axis_index("head") * column_width, column_width, 1
    )
    piece = lax.all_gather(tokens, "head", axis=1, tiled=True)
    rows_flat = piece.reshape(-1, model_width)
    result = jnp.dot(rows_flat, columns, precision=highest, preferred_element_type=jnp.float32)
    packed = result.reshape(piece.shape[0], piece.shape[1], column_width)
    local_rows = local_frames * frame_tokens
    packed = packed.reshape(local_rows, local_heads, 3 * head_dim)
    query_mask = (jnp.arange(2 * head_dim, dtype=jnp.int32) < head_dim).astype(jnp.float32)
    queries = (packed[:, :, : 2 * head_dim] * query_mask).reshape(
        -1, BLOCK, local_heads, 2 * head_dim
    )
    own_pairs = packed[:, :, head_dim:].reshape(local_rows, local_heads * 2 * head_dim)
    all_pairs = lax.all_gather(own_pairs, "frame", axis=0, tiled=True)
    all_pairs = all_pairs.reshape(-1, BLOCK, local_heads, 2 * head_dim)
    local_blocks = queries.shape[0]
    group_blocks = math.gcd(local_blocks, max(1, 512 // BLOCK))
    group_count = local_blocks // group_blocks
    factor = head_dim ** (-0.5)
    grouped = (
        queries.reshape(group_count, group_blocks, BLOCK, local_heads, 2 * head_dim),
        block_lists.reshape(group_count, group_blocks, -1),
        block_counts.reshape(group_count, group_blocks),
    )

    def one_group(items):
        return attend_padded(items[0], all_pairs, items[1], items[2], factor)

    attended = lax.map(one_group, grouped)
    attended = attended.reshape(local_frames, head_groups, strip_tokens, local_heads * head_dim)
    attended = lax.all_to_all(attended, "head", split_axis=1, concat_axis=3, tiled=True)
    attended = attended.reshape(-1, model_width)
    stream = flat_strip + jnp.dot(
        attended, out_weight, precision=highest, preferred_element_type=jnp.float32
    )
    normed = layer_norm(stream, norm_gain)
    features = jnp.dot(
        normed, proj_weight, precision=highest, preferred_element_type=jnp.float32
    ).astype(jnp.bfloat16)
    channels = features.shape[1]
    strip_rows = strip_tokens // GRID
    lifted = jnp.dot(features, up_weight, preferred_element_type=jnp.float32).astype(jnp.bfloat16)
    lifted = lifted.reshape(local_frames, strip_rows, GRID, 4, 4, channels)
    upsampled = jnp.transpose(lifted, (0, 1, 3, 2, 4, 5)).reshape(
        local_frames, 4 * strip_rows, 4 * GRID, channels
    )
    activated = jnp.maximum(upsampled, jnp.zeros((), jnp.bfloat16))
    rimmed = extended_2(activated, (("head", 1),), 1)
    first_conv = conv_window(pad_columns(rimmed), conv_weight[0]) + conv_bias[0]
    hidden = jnp.maximum(first_conv, 0.0).astype(jnp.bfloat16)
    extended = extended_2(hidden, (("head", 1),), 1)
    second = conv_window(pad_columns(extended), conv_weight[1]) + conv_bias[1]
    return (upsampled.astype(jnp.float32) + second).astype(jnp.bfloat16)


def solution(mesh):
    in_specs = (
        P("frame", "head", None),
        P(),
        P(),
        P(),
        P(),
        P(),
        P(),
        P(),
        P("frame", None),
        P("frame"),
    )
    out_specs = P("frame", "head", None, None)
    return jax.shard_map(
        on_device, mesh=mesh, in_specs=in_specs, out_specs=out_specs, check_vma=False
    )
```

profile of v0, /device:TPU:1, one launch (start us, length us, event | category | flops | bytes accessed | tf_op | source)
XLA Modules:
  0.0 552.1 jit_solution(14968831860393375033)
XLA Ops:
  7.3 86.2 %all-gather.3.cloned.1.call-done = f32[2,1024,1024]{2,1,0:T(8,128)} async-done(((f32[2,128,1024]{2,1,0:T(8,128)}), f32[2,1024,1024]{2,1,0:T(8,128)}) %all-gather.3.cloned.1.call-update) | async-done | bytes 8388624 | tf_op jit(solution)/shard_map/all_gather | solution.py:93
  93.5 22.6 %fusion.26 = f32[384,2048]{1,0:T(8,128)S(1)} fusion(f32[2048,1024]{1,0:T(8,128)} %bitcast.179, f32[1024,3072]{1,0:T(8,128)} %param.13, s32[]{:T(128)S(6)} %select_n.35), kind=kOutput, calls=%fused_computation.69 | convolution fusion | flops 9663676416 | bytes 13107204 | tf_op jit(solution)/shard_map/dot_general | solution.py:95
  116.1 2.5 fusion.41
  118.6 2.9 copy.60
  122.3 2.9 copy.78
  125.1 3.1 broadcast_multiply_fusion
  128.2 78.9 %all-gather.5.cloned.1.call-done = f32[8192,256]{1,0:T(8,128)} async-done(((f32[2048,256]{1,0:T(8,128)}), f32[8192,256]{1,0:T(8,128)}) %all-gather.5.cloned.1.call-update) | async-done | bytes 8388624 | tf_op jit(solution)/shard_map/all_gather | solution.py:104
  207.1 10.9 %reshape.206 = f32[64,128,2,128]{3,2,1,0:T(2,128)} reshape(f32[8192,256]{1,0:T(8,128)} %all-gather.5.cloned.1.call-done) | data formatting | bytes 16777216 | tf_op jit(solution)/shard_map/reshape | solution.py:105
  218.0 185.2 %while.12 = (s32[]{:T(128)}, f32[4,4,128,2,64]{2,4,3,1,0:T(8,128)S(1)}, s32[4,4,13]{2,1,0:T(4,128)}, f32[64,128,2,128]{3,2,1,0:T(2,128)}, s32[4,4]{1,0:T(4,128)S(1)}, /*index=5*/f32[4,4,128,2,128]{4,2,1,0,3:T(8,128)}, s32[]{:T(128)}) while((s32[]{:T(128)}, f32[4,4,128,2,64]{2,4,3,1,0:T(8,128)S(1)}, s32[4,4,13]{2,1,0:T(4,128)}, ...), condition=%wide.region_3.4_spmd, body=%wide.region_0.3_spmd.sunk | while | flops 5251615744 | bytes 90243968 | solution.py:119
  219.1 14.2 %gather_fusion = f32[52,128,2,128]{3,2,1,0:T(2,128)} fusion(f32[64,128,2,128]{3,2,1,0:T(2,128)} %get-tuple-element.210, s32[1024]{0:T(1024)S(1)} %pad_clamp_fusion.2), kind=kCustom, calls=%fused_computation.clone.1 | custom fusion | bytes 13631696 | tf_op jit(solution)/shard_map/while/body/eval_jaxpr/gather | solution.py:31
  233.2 11.1 %copy.95 = f32[4,1664,2,128]{1,3,2,0:T(8,128)} copy(f32[4,1664,2,128]{3,2,1,0:T(2,128)} %bitcast.165) | data formatting | bytes 13631488 | tf_op jit(solution)/shard_map/while/body/eval_jaxpr/reshape | solution.py:32
  244.4 9.0 %fusion.82 = (f32[4,2,128]{2,1,0:T(2,128)S(1)}, f32[4,2,128,1664]{3,2,1,0:T(8,128)S(1)}) fusion(pred[4,1664]{1,0:T(4,128)(4,1)S(1)} %broadcast_compare_fusion.2, f32[4,1664,2,128]{1,3,2,0:T(8,128)} %copy.95, f32[4,4,128,2,128]{4,2,1,0,3:T(8,128)} %get-tuple-element.212, s32[]{:T(128)} %get-tuple-element.200), kind=kOutput, calls=%fused_computation.3.clone.1 | convolution fusion | flops 2622356480 | bytes 14167040 | tf_op jit(solution)/shard_map/while/body/eval_jaxpr/gihe,gjhe->ghij/dot_general | solution.py:33
  253.5 1.5 fusion.84
  254.9 1.4 copy-done.2
  256.4 8.0 %fusion.83 = f32[4,128,2,128]{1,3,2,0:T(8,128)S(1)} fusion(f32[4,1664,2,128]{1,3,2,0:T(8,128)S(1)} %copy-done.2, f32[4,2,128,1664]{3,2,1,0:T(8,128)S(1)} %get-tuple-element.191, f32[4,2,128]{2,1,0:T(2,128)S(1)} %get-tuple-element.192, pred[4,1664]{1,0:T(4,128)(4,1)S(1)} %broadcast_compare_fusion.2), kind=kOutput, calls=%fused_computation.10.clone.1 | convolution fusion | flops 2622357504 | bytes 14166528 | tf_op jit(solution)/shard_map/while/body/eval_jaxpr/ghij,gjhe->gihe/dot_general | solution.py:40
  265.3 14.2 %gather_fusion = f32[52,128,2,128]{3,2,1,0:T(2,128)} fusion(f32[64,128,2,128]{3,2,1,0:T(2,128)} %get-tuple-element.210, s32[1024]{0:T(1024)S(1)} %pad_clamp_fusion.2), kind=kCustom, calls=%fused_computation.clone.1 | custom fusion | bytes 13631696 | tf_op jit(solution)/shard_map/while/body/eval_jaxpr/gather | solution.py:31
  279.4 11.1 %copy.95 = f32[4,1664,2,128]{1,3,2,0:T(8,128)} copy(f32[4,1664,2,128]{3,2,1,0:T(2,128)} %bitcast.165) | data formatting | bytes 13631488 | tf_op jit(solution)/shard_map/while/body/eval_jaxpr/reshape | solution.py:32
  290.6 9.0 %fusion.82 = (f32[4,2,128]{2,1,0:T(2,128)S(1)}, f32[4,2,128,1664]{3,2,1,0:T(8,128)S(1)}) fusion(pred[4,1664]{1,0:T(4,128)(4,1)S(1)} %broadcast_compare_fusion.2, f32[4,1664,2,128]{1,3,2,0:T(8,128)} %copy.95, f32[4,4,128,2,128]{4,2,1,0,3:T(8,128)} %get-tuple-element.212, s32[]{:T(128)} %get-tuple-element.200), kind=kOutput, calls=%fused_computation.3.clone.1 | convolution fusion | flops 2622356480 | bytes 14167040 | tf_op jit(solution)/shard_map/while/body/eval_jaxpr/gihe,gjhe->ghij/dot_general | solution.py:33
  299.6 1.5 fusion.84
  301.1 1.4 copy-done.2
  302.6 8.0 %fusion.83 = f32[4,128,2,128]{1,3,2,0:T(8,128)S(1)} fusion(f32[4,1664,2,128]{1,3,2,0:T(8,128)S(1)} %copy-done.2, f32[4,2,128,1664]{3,2,1,0:T(8,128)S(1)} %get-tuple-element.191, f32[4,2,128]{2,1,0:T(2,128)S(1)} %get-tuple-element.192, pred[4,1664]{1,0:T(4,128)(4,1)S(1)} %broadcast_compare_fusion.2), kind=kOutput, calls=%fused_computation.10.clone.1 | convolution fusion | flops 2622357504 | bytes 14166528 | tf_op jit(solution)/shard_map/while/body/eval_jaxpr/ghij,gjhe->gihe/dot_general | solution.py:40
  311.4 14.2 %gather_fusion = f32[52,128,2,128]{3,2,1,0:T(2,128)} fusion(f32[64,128,2,128]{3,2,1,0:T(2,128)} %get-tuple-element.210, s32[1024]{0:T(1024)S(1)} %pad_clamp_fusion.2), kind=kCustom, calls=%fused_computation.clone.1 | custom fusion | bytes 13631696 | tf_op jit(solution)/shard_map/while/body/eval_jaxpr/gather | solution.py:31
  325.6 11.1 %copy.95 = f32[4,1664,2,128]{1,3,2,0:T(8,128)} copy(f32[4,1664,2,128]{3,2,1,0:T(2,128)} %bitcast.165) | data formatting | bytes 13631488 | tf_op jit(solution)/shard_map/while/body/eval_jaxpr/reshape | solution.py:32
  336.8 9.0 %fusion.82 = (f32[4,2,128]{2,1,0:T(2,128)S(1)}, f32[4,2,128,1664]{3,2,1,0:T(8,128)S(1)}) fusion(pred[4,1664]{1,0:T(4,128)(4,1)S(1)} %broadcast_compare_fusion.2, f32[4,1664,2,128]{1,3,2,0:T(8,128)} %copy.95, f32[4,4,128,2,128]{4,2,1,0,3:T(8,128)} %get-tuple-element.212, s32[]{:T(128)} %get-tuple-element.200), kind=kOutput, calls=%fused_computation.3.clone.1 | convolution fusion | flops 2622356480 | bytes 14167040 | tf_op jit(solution)/shard_map/while/body/eval_jaxpr/gihe,gjhe->ghij/dot_general | solution.py:33
  345.8 1.5 fusion.84
  347.3 1.4 copy-done.2
  348.7 8.0 %fusion.83 = f32[4,128,2,128]{1,3,2,0:T(8,128)S(1)} fusion(f32[4,1664,2,128]{1,3,2,0:T(8,128)S(1)} %copy-done.2, f32[4,2,128,1664]{3,2,1,0:T(8,128)S(1)} %get-tuple-element.191, f32[4,2,128]{2,1,0:T(2,128)S(1)} %get-tuple-element.192, pred[4,1664]{1,0:T(4,128)(4,1)S(1)} %broadcast_compare_fusion.2), kind=kOutput, calls=%fused_computation.10.clone.1 | convolution fusion | flops 2622357504 | bytes 14166528 | tf_op jit(solution)/shard_map/while/body/eval_jaxpr/ghij,gjhe->gihe/dot_general | solution.py:40
  357.6 14.2 %gather_fusion = f32[52,128,2,128]{3,2,1,0:T(2,128)} fusion(f32[64,128,2,128]{3,2,1,0:T(2,128)} %get-tuple-element.210, s32[1024]{0:T(1024)S(1)} %pad_clamp_fusion.2), kind=kCustom, calls=%fused_computation.clone.1 | custom fusion | bytes 13631696 | tf_op jit(solution)/shard_map/while/body/eval_jaxpr/gather | solution.py:31
  371.7 11.1 %copy.95 = f32[4,1664,2,128]{1,3,2,0:T(8,128)} copy(f32[4,1664,2,128]{3,2,1,0:T(2,128)} %bitcast.165) | data formatting | bytes 13631488 | tf_op jit(solution)/shard_map/while/body/eval_jaxpr/reshape | solution.py:32
  382.9 9.0 %fusion.82 = (f32[4,2,128]{2,1,0:T(2,128)S(1)}, f32[4,2,128,1664]{3,2,1,0:T(8,128)S(1)}) fusion(pred[4,1664]{1,0:T(4,128)(4,1)S(1)} %broadcast_compare_fusion.2, f32[4,1664,2,128]{1,3,2,0:T(8,128)} %copy.95, f32[4,4,128,2,128]{4,2,1,0,3:T(8,128)} %get-tuple-element.212, s32[]{:T(128)} %get-tuple-element.200), kind=kOutput, calls=%fused_computation.3.clone.1 | convolution fusion | flops 2622356480 | bytes 14167040 | tf_op jit(solution)/shard_map/while/body/eval_jaxpr/gihe,gjhe->ghij/dot_general | solution.py:33
  392.0 1.5 fusion.84
  393.4 1.4 copy-done.2
  394.9 8.0 %fusion.83 = f32[4,128,2,128]{1,3,2,0:T(8,128)S(1)} fusion(f32[4,1664,2,128]{1,3,2,0:T(8,128)S(1)} %copy-done.2, f32[4,2,128,1664]{3,2,1,0:T(8,128)S(1)} %get-tuple-element.191, f32[4,2,128]{2,1,0:T(2,128)S(1)} %get-tuple-element.192, pred[4,1664]{1,0:T(4,128)(4,1)S(1)} %broadcast_compare_fusion.2), kind=kOutput, calls=%fused_computation.10.clone.1 | convolution fusion | flops 2622357504 | bytes 14166528 | tf_op jit(solution)/shard_map/while/body/eval_jaxpr/ghij,gjhe->gihe/dot_general | solution.py:40
  403.1 1.3 copy.63
  404.4 5.4 all-to-all-start
  409.9 2.8 slice_bitcast_fusion
  412.7 22.9 %all-to-all-done = f32[2,8,128,128]{3,2,0,1:T(8,128)} async-done(((f32[2,8,128,128]{3,2,0,1:T(8,128)}), f32[2,8,128,128]{3,2,0,1:T(8,128)}, u32[]{:S(2)}, u32[]{:S(2)}) %all-to-all-start) | async-done | bytes 1048608 | tf_op jit(solution)/shard_map/all_to_all | solution.py:121
  435.6 1.9 copy.64
  437.5 6.2 %fusion.47 = (f32[256]{0:T(256)S(1)}, f32[256,1024]{1,0:T(8,128)S(1)}) fusion(f32[256,1024]{1,0:T(8,128)S(1)} %bitcast.194, f32[1024,1024]{1,0:T(8,128)} %param.14, f32[32,8,8,128]{3,2,1,0:T(8,128)S(1)} %bitcast.195), kind=kOutput, calls=%fused_computation.118 | convolution fusion | flops 3221749504 | bytes 7341056 | tf_op jit(solution)/shard_map/dot_general | solution.py:123
  444.0 1.1 convolution_convert_fusion.1
  445.2 2.7 broadcast_maximum_fusion
  447.9 4.5 max.34
  452.4 5.0 copy.67
  457.4 0.9 fusion.45
  458.3 1.9 collective-permute-start
  460.2 2.4 collective-permute-start.1
  462.6 2.5 copy.91
  465.1 4.2 max.37
  469.3 5.8 %pad_maximum_fusion.2 = (bf16[2,16,128,256]{3,0,2,1:T(2,128)(2,1)S(1)}, bf16[2,16,128,256]{3,0,2,1:T(2,128)(2,1)S(1)}) fusion(bf16[2,1,128,256]{3,0,2,1:T(2,128)(2,1)S(1)} %collective-permute-done.1, bf16[2,16,128,256]{3,0,2,1:T(2,128)(2,1)S(1)} %bitcast.168, bf16[2,1,128,256]{3,0,2,1:T(2,128)(2,1)S(1)} %collective-permute-done), kind=kLoop, calls=%fused_computation.64 | loop fusion | flops 2097152 | bytes 6553600 | tf_op jit(solution)/shard_map/concatenate | solution.py:23
  475.5 4.2 select_maximum_fusion
  479.7 10.9 %fusion.43 = (bf16[2,16,128,256]{3,0,2,1:T(2,128)(2,1)S(1)}, bf16[2,16,128,256]{3,0,2,1:T(2,128)(2,1)S(1)}, bf16[2,16,128,256]{3,0,2,1:T(2,128)(2,1)S(1)}, bf16[...) fusion(bf16[2,18,130,256]{3,0,2,1:T(2,128)(2,1)S(1)} %select_maxim, ...), kind=kLoop, calls=%fused_computation.114 | loop fusion | bytes 25165824 | tf_op jit(solution)/shard_map/slice | solution.py:58
  493.4 0.9 copy-done.8
  502.3 1.4 copy-done.3
  504.4 3.1 collective-permute-start.2
  507.6 1.9 collective-permute-start.3
  509.5 6.4 %reshape.229 = f32[2,4,32,4,4,256]{5,4,3,2,1,0:T(4,128)} reshape(bf16[256,4096]{1,0:T(8,128)(2,1)} %get-tuple-element.151) | data formatting | bytes 6291456 | tf_op jit(solution)/shard_map/convert_element_type | solution.py:143
  515.9 5.3 copy.65
  521.2 5.4 reshape.228
  526.6 1.1 fusion.23
  527.7 5.2 fusion.42
  536.0 1.5 copy-done.4
  540.4 0.8 fusion.17
  541.2 1.3 copy-done.6
  542.5 2.2 add_convert_fusion
  (97 shorter events, 23.2 us)
Async XLA Ops:
  6.5 438.6 %copy-start = (bf16[256,4096]{1,0:T(8,128)(2,1)S(1)}, bf16[256,4096]{1,0:T(8,128)(2,1)}, u32[]{:S(2)}) copy-start(bf16[256,4096]{1,0:T(8,128)(2,1)} %param.17) | copy-start | bytes 6291460
  6.5 86.9 %all-gather.3.cloned.1.call-start = ((), (), s32[]{:S(2)}) async-start(), calls=%async_computation.1 | async-start | bytes 9437184 | tf_op jit(solution)/shard_map/all_gather | solution.py:93
  7.3 199.8 %all-gather.5.cloned.1.call-start = ((), (), s32[]{:S(2)}) async-start(), calls=%async_computation.2 | async-start | bytes 10485760 | tf_op jit(solution)/shard_map/all_gather | solution.py:104
  121.5 0.7 copy-start.13
  253.5 2.9 copy-start.2
  299.6 2.9 copy-start.2
  345.8 2.9 copy-start.2
  392.0 2.9 copy-start.2
  404.4 31.1 %all-to-all-start = ((f32[2,8,128,128]{3,2,0,1:T(8,128)}), f32[2,8,128,128]{3,2,0,1:T(8,128)}, u32[]{:S(2)}, u32[]{:S(2)}) async-start(f32[2,8,128,128]{3,2,0,1:T(8,128)} %copy.63), calls=%async_computation | async-start | bytes 2097152 | tf_op jit(solution)/shard_map/all_to_all | solution.py:121
  435.6 1.9 copy-start.9
  437.5 6.5 %copy-start.10 = (f32[1024,256]{1,0:T(8,128)S(1)}, f32[1024,256]{1,0:T(8,128)}, u32[]{:S(2)}) copy-start(f32[1024,256]{1,0:T(8,128)} %param.16) | copy-start | bytes 3145732
  437.5 6.5 %copy-start.11 = (f32[1024]{0:T(1024)S(1)}, f32[1024]{0:T(1024)}, u32[]{:S(2)}) copy-start(f32[1024]{0:T(1024)} %param.15) | copy-start | bytes 12292
  452.4 10.2 %copy-start.12 = (f32[2,256]{1,0:T(2,128)S(1)}, f32[2,256]{1,0:T(2,128)}, u32[]{:S(2)}) copy-start(f32[2,256]{1,0:T(2,128)} %param.19) | copy-start | bytes 6148
  452.4 10.2 %copy-start.5 = (bf16[2,4,32,4,4,256]{5,4,3,2,1,0:T(4,128)(2,1)S(1)}, bf16[2,4,32,4,4,256]{5,4,3,2,1,0:T(4,128)(2,1)}, u32[]{:S(2)}) copy-start(bf16[2,4,32,4,4,256]{5,4,3,2,1,0:T(4,128)(2,1)} %max.34) | copy-start | bytes 6291460
  458.3 11.0 %collective-permute-start = (bf16[2,1,128,256]{3,0,2,1:T(2,128)(2,1)}, bf16[2,1,128,256]{3,0,2,1:T(2,128)(2,1)S(1)}, u32[]{:S(2)}, u32[]{:S(2)}) collective-permute-start(bf16[2,1,128,256]{3,0,2,1:T(2,128)(2,1)} %get-tuple-element.144), channel_id=1, source_target_pairs={{0,1},{1,2},{2,3},{3,4},{4,5},{5,6},{6,7},{8,9},{9,10},{10,11},{11... | collective-permute-start | bytes 393224 | tf_op jit(solution)/shard_map/ppermute | solution.py:19
  460.2 9.1 %collective-permute-start.1 = (bf16[2,1,128,256]{3,0,2,1:T(2,128)(2,1)}, bf16[2,1,128,256]{3,0,2,1:T(2,128)(2,1)S(1)}, u32[]{:S(2)}, u32[]{:S(2)}) collective-permute-start(bf16[2,1,128,256]{3,0,2,1:T(2,128)(2,1)} %get-tuple-element.145), channel_id=1, source_target_pairs={{1,0},{2,1},{3,2},{4,3},{5,4},{6,5},{7,6},{9,8},{10,9},{11,10},{12... | collective-permute-start | bytes 393224 | tf_op jit(solution)/shard_map/ppermute | solution.py:22
  493.0 1.3 copy-start.8
  496.5 1.6 copy-start.7
  501.8 2.0 copy-start.3
  504.4 22.1 %collective-permute-start.2 = (bf16[2,1,128,256]{3,2,1,0:T(8,128)(2,1)}, bf16[2,1,128,256]{3,2,1,0:T(8,128)(2,1)S(1)}, u32[]{:S(2)}, u32[]{:S(2)}) collective-permute-start(bf16[2,1,128,256]{3,2,1,0:T(8,128)(2,1)} %get-tuple-element.140), channel_id=1, source_target_pairs={{0,1},{1,2},{2,3},{3,4},{4,5},{5,6},{6,7},{8,9},{9,10},{10,11},{11... | collective-permute-start | bytes 393224 | tf_op jit(solution)/shard_map/ppermute | solution.py:19
  507.6 19.0 %collective-permute-start.3 = (bf16[2,1,128,256]{3,2,1,0:T(8,128)(2,1)}, bf16[2,1,128,256]{3,2,1,0:T(8,128)(2,1)S(1)}, u32[]{:S(2)}, u32[]{:S(2)}) collective-permute-start(bf16[2,1,128,256]{3,2,1,0:T(8,128)(2,1)} %get-tuple-element.141), channel_id=1, source_target_pairs={{1,0},{2,1},{3,2},{4,3},{5,4},{6,5},{7,6},{9,8},{10,9},{11,10},{12... | collective-permute-start | bytes 393224 | tf_op jit(solution)/shard_map/ppermute | solution.py:22
  535.3 2.2 copy-start.4
  540.3 2.2 copy-start.6
  542.5 2.2 copy-start.1
Sparse Core Ops, SparseCore 0:
  8.9 84.4 all-gather.2
  121.7 85.3 all-gather.4
where the time goes:
time: 563 us; the launch traced here: 552 us
  local copies, waits for them, and re-layouts  193 us (34%)
  waiting for transfers between devices  189 us (34%)
  matrix products  114 us (20%)
  other arithmetic  26.7 us (5%)
  starting transfers between devices  14.9 us (3%)
  between operations  14.3 us (3%)
    all_gather x1, waiting for transfers between devices, on_device(): piece = lax.all_gather(tokens, 'head', axis=1, tiled=True)  86.2 us
    all_gather x1, waiting for transfers between devices, on_device(): all_pairs = lax.all_gather(own_pairs, 'frame', axis=0, tiled=True)  78.9 us
    gather x4, local copies, waits for them, and re-layouts, attend_padded(): picked = key_values[block_ids]  56.6 us
    reshape x4, local copies, waits for them, and re-layouts, attend_padded(): picked.reshape((groups, slot_total * block_size) + picked.shape[3:])  44.4 us
    dot_general x4, matrix products, attend_padded(): jnp.einsum('gihe,gjhe->ghij', queries, picked, precision=highest) * factor  36.1 us
    dot_general x4, matrix products, attend_padded(): blended = jnp.einsum('ghij,gjhe->gihe', weights, picked, precision=highest)  32.1 us
    all_to_all x1, waiting for transfers between devices, on_device(): lax.all_to_all(attended, 'head', split_axis=1, concat_axis=3, tiled=True)  22.9 us
    dot_general x1, matrix products, on_device(): jnp.dot(rows_flat, columns, precision=highest, preferred_element_type=jnp...  22.6 us
  transfers between devices with their start and end apart: 7, of which 3 were waited for; matrix products, arithmetic and copies ran while one was open for 6% of the time, Pallas kernels for 0%

commit v1 on v0

--- a/solution.py
+++ b/solution.py
@@ -9,6 +9,17 @@
 BLOCK = 128
 highest = lax.Precision.HIGHEST
 eps_norm = 1e-05
+
+
+def gather_by_hops(x, axis, dim):
+    size = lax.axis_size(axis)
+    route = [(i, (i + 1) % size) for i in range(size)]
+    parts = [x]
+    for far in range(1, size):
+        parts = [lax.ppermute(parts[0], axis, route), *parts]
+    whole = jnp.concatenate(parts, axis=dim)
+    shift = (lax.axis_index(axis) + 1) * parts[-1].shape[dim]
+    return jnp.roll(whole, shift, axis=dim)
 
 
 def extended_2(block, sides, width):
@@ -90,7 +101,7 @@
     columns = lax.dynamic_slice_in_dim(
         qkv_weight, lax.axis_index("head") * column_width, column_width, 1
     )
-    piece = lax.all_gather(tokens, "head", axis=1, tiled=True)
+    piece = gather_by_hops(tokens, "head", 1)
     rows_flat = piece.reshape(-1, model_width)
     result = jnp.dot(rows_flat, columns, precision=highest, preferred_element_type=jnp.float32)
     packed = result.reshape(piece.shape[0], piece.shape[1], column_width)

time: 563 us -> 624 us (1.11)
  local copies, waits for them, and re-layouts: 193 us -> 231 us
  starting transfers between devices: 14.9 us -> 32.9 us
    all_gather x1 -> x0, waiting for transfers between devices: 86.2 us -> none  [on_device(): piece = lax.all_gather(tokens, 'head', axis=1, tiled=True)]
    ppermute x0 -> x7, waiting for transfers between devices: none -> 77.1 us  [gather_by_hops(): parts = [lax.ppermute(parts[0], axis, route), *parts]]
    unnamed x27 -> x64, local copies, waits for them, and re-layouts: 9.38 us -> 39.3 us
    ppermute x0 -> x7, starting transfers between devices: none -> 17.6 us  [gather_by_hops(): parts = [lax.ppermute(parts[0], axis, route), *parts]]
    all_gather x1, waiting for transfers between devices: 78.9 us -> 95.2 us  [on_device(): all_pairs = lax.all_gather(own_pairs, 'frame', axis=0, tiled=True)]
    dot_general x1, matrix products: 22.6 us -> 10.7 us  [on_device(): jnp.dot(rows_flat, columns, precision=highest, preferred_element_type=jnp...]
    dynamic_slice x0 -> x9, local copies, waits for them, and re-layouts: none -> 9.53 us  [the longest x8 5.18 us: on_device(): attended = lax.map(one_group, grouped)]
    dot_general x4, matrix products: 32.1 us -> 40.7 us  [attend_padded(): blended = jnp.einsum('ghij,gjhe->gihe', weights, picked, precision=highest)]
  transfers between devices with their start and end apart: 7 -> 13, of which waited for: 3 -> 9; matrix products, arithmetic and copies ran while one was open for 6% -> 6% of each run, Pallas kernels for 0% -> 0%
where the time goes in v1:
time: 624 us; the launch traced here: 612 us
  local copies, waits for them, and re-layouts  231 us (37%)
  waiting for transfers between devices  195 us (31%)
  matrix products  110 us (18%)
  starting transfers between devices  32.9 us (5%)
  other arithmetic  28.9 us (5%)
  between operations  14.3 us (2%)
    all_gather x1, waiting for transfers between devices, on_device(): all_pairs = lax.all_gather(own_pairs, 'frame', axis=0, tiled=True)  95.2 us
    ppermute x7, waiting for transfers between devices, gather_by_hops(): parts = [lax.ppermute(parts[0], axis, route), *parts]  77.1 us
    gather x4, local copies, waits for them, and re-layouts, attend_padded(): picked = key_values[block_ids]  56.7 us
    reshape x4, local copies, waits for them, and re-layouts, attend_padded(): picked.reshape((groups, slot_total * block_size) + picked.shape[3:])  44.3 us
    dot_general x4, matrix products, attend_padded(): blended = jnp.einsum('ghij,gjhe->gihe', weights, picked, precision=highest)  40.7 us
    unnamed x64, local copies, waits for them, and re-layouts  39.3 us
    dot_general x4, matrix products, attend_padded(): jnp.einsum('gihe,gjhe->ghij', queries, picked, precision=highest) * factor  35.7 us
    all_to_all x1, waiting for transfers between devices, on_device(): lax.all_to_all(attended, 'head', split_axis=1, concat_axis=3, tiled=True)  22.4 us
  transfers between devices with their start and end apart: 13, of which 9 were waited for; matrix products, arithmetic and copies ran while one was open for 6% of the time, Pallas kernels for 0%

profile of v1, /device:TPU:1, one launch (start us, length us, event | category | flops | bytes accessed | tf_op | source)
XLA Modules:
  0.0 612.4 jit_solution(16294469498394150457)
XLA Ops:
  6.5 2.7 collective-permute-start
  9.2 12.1 %collective-permute-done = f32[2,128,1024]{2,1,0:T(8,128)S(1)} collective-permute-done((f32[2,128,1024]{2,1,0:T(8,128)}, f32[2,128,1024]{2,1,0:T(8,128)S(1)}, u32[]{:S(2)}, u32[]{:S(2)}) %collective-permute-start) | collective-permute-done | bytes 1048608 | tf_op jit(solution)/shard_map/ppermute | solution.py:19
  21.3 2.4 collective-permute-start.1
  23.7 11.7 %collective-permute-done.1 = f32[2,128,1024]{2,1,0:T(8,128)S(1)} collective-permute-done((f32[2,128,1024]{2,1,0:T(8,128)S(1)}, f32[2,128,1024]{2,1,0:T(8,128)S(1)}, u32[]{:S(2)}, u32[]{:S(2)}) %collective-permute-start.1) | collective-permute-done | bytes 1048608 | tf_op jit(solution)/shard_map/ppermute | solution.py:19
  36.4 2.5 collective-permute-start.2
  38.8 11.7 %collective-permute-done.2 = f32[2,128,1024]{2,1,0:T(8,128)S(1)} collective-permute-done((f32[2,128,1024]{2,1,0:T(8,128)S(1)}, f32[2,128,1024]{2,1,0:T(8,128)S(1)}, u32[]{:S(2)}, u32[]{:S(2)}) %collective-permute-start.2) | collective-permute-done | bytes 1048608 | tf_op jit(solution)/shard_map/ppermute | solution.py:19
  51.6 2.5 collective-permute-start.3
  54.1 11.7 %collective-permute-done.3 = f32[2,128,1024]{2,1,0:T(8,128)S(1)} collective-permute-done((f32[2,128,1024]{2,1,0:T(8,128)S(1)}, f32[2,128,1024]{2,1,0:T(8,128)S(1)}, u32[]{:S(2)}, u32[]{:S(2)}) %collective-permute-start.3) | collective-permute-done | bytes 1048608 | tf_op jit(solution)/shard_map/ppermute | solution.py:19
  66.8 2.5 collective-permute-start.4
  69.3 11.7 %collective-permute-done.4 = f32[2,128,1024]{2,1,0:T(8,128)S(1)} collective-permute-done((f32[2,128,1024]{2,1,0:T(8,128)S(1)}, f32[2,128,1024]{2,1,0:T(8,128)S(1)}, u32[]{:S(2)}, u32[]{:S(2)}) %collective-permute-start.4) | collective-permute-done | bytes 1048608 | tf_op jit(solution)/shard_map/ppermute | solution.py:19
  82.0 2.5 collective-permute-start.5
  84.5 11.7 %collective-permute-done.5 = f32[2,128,1024]{2,1,0:T(8,128)} collective-permute-done((f32[2,128,1024]{2,1,0:T(8,128)S(1)}, f32[2,128,1024]{2,1,0:T(8,128)}, u32[]{:S(2)}, u32[]{:S(2)}) %collective-permute-start.5) | collective-permute-done | bytes 1048608 | tf_op jit(solution)/shard_map/ppermute | solution.py:19
  96.2 2.6 collective-permute-start.6
  98.8 2.7 dynamic-slice_bitcast_fusion
  101.5 3.1 copy.62
  104.5 6.3 %collective-permute-done.6 = f32[2,128,1024]{2,1,0:T(8,128)} collective-permute-done((f32[2,128,1024]{2,1,0:T(8,128)}, f32[2,128,1024]{2,1,0:T(8,128)}, u32[]{:S(2)}, u32[]{:S(2)}) %collective-permute-start.6) | collective-permute-done | bytes 1048608 | tf_op jit(solution)/shard_map/ppermute | solution.py:19
  110.9 2.3 constant_dynamic-update-slice_fusion.15
  113.2 2.4 constant_dynamic-update-slice_fusion.14
  122.1 2.3 constant_dynamic-update-slice_fusion.7
  124.4 2.3 constant_dynamic-update-slice_fusion.6
  133.2 4.3 constant_dynamic-slice_fusion.2
  137.5 10.7 %fusion.45 = f32[2048,2,192]{0,2,1:T(8,128)S(1)} fusion(f32[2048,1024,1]{1,0,2:T(8,128)S(1)} %bitcast.176, f32[2,192,1024]{2,1,0:T(8,128)S(1)} %bitcast.204), kind=kOutput, calls=%fused_computation.133 | convolution fusion | flops 9663676416 | bytes 13107200 | tf_op jit(solution)/shard_map/dot_general | solution.py:106
  148.2 2.5 slice_multiply_fusion
  150.8 3.6 reshape_reshape.4
  154.5 95.2 %all-gather.2.cloned.1.call-done = f32[8192,256]{0,1:T(8,128)} async-done(((f32[2048,256]{0,1:T(8,128)}), f32[8192,256]{0,1:T(8,128)}) %all-gather.2.cloned.1.call-update) | async-done | bytes 8388624 | tf_op jit(solution)/shard_map/all_gather | solution.py:115
  249.6 8.3 %copy.81 = f32[32,8,64,128]{3,2,1,0:T(8,128)} copy(f32[32,8,64,128]{3,1,2,0:T(8,128)} %bitcast.189) | data formatting | bytes 16777216
  257.9 10.0 %copy.78 = f32[64,128,2,128]{3,2,1,0:T(2,128)} copy(f32[64,128,2,128]{1,0,3,2:T(8,128)} %bitcast.177) | data formatting | bytes 16777216 | tf_op jit(solution)/shard_map/reshape | solution.py:116
  267.9 195.2 %while.12 = (s32[]{:T(128)}, f32[4,4,128,2,64]{2,4,3,1,0:T(8,128)}, s32[4,4,13]{2,1,0:T(4,128)}, f32[64,128,2,128]{3,2,1,0:T(2,128)}, s32[4,4]{1,0:T(4,128)S(1)}, /*index=5*/f32[4,4,128,2,128]{2,1,0,4,3:T(4,128)}, s32[]{:T(128)}) while((s32[]{:T(128)}, f32[4,4,128,2,64]{2,4,3,1,0:T(8,128)}, s32[4,4,13]{2,1,0:T(4,128)}, ...), condition=%wide.region_3.4_spmd, body=%wide.region_0.3_spmd.sunk | while | flops 5251615744 | bytes 65078120 | solution.py:130
  268.7 14.2 %gather_fusion = f32[52,128,2,128]{3,2,1,0:T(2,128)} fusion(f32[64,128,2,128]{3,2,1,0:T(2,128)} %get-tuple-element.216, s32[1024]{0:T(1024)S(1)} %pad_clamp_fusion.2), kind=kCustom, calls=%fused_computation.clone.1 | custom fusion | bytes 13631696 | tf_op jit(solution)/shard_map/while/body/eval_jaxpr/gather | solution.py:42
  282.9 11.1 %copy.93 = f32[4,1664,2,128]{1,3,2,0:T(8,128)} copy(f32[4,1664,2,128]{3,2,1,0:T(2,128)} %bitcast.174) | data formatting | bytes 13631488 | tf_op jit(solution)/shard_map/while/body/eval_jaxpr/reshape | solution.py:43
  295.3 8.9 %fusion.81 = (f32[4,2,128]{2,1,0:T(2,128)S(1)}, f32[4,2,128,1664]{3,2,1,0:T(8,128)S(1)}) fusion(pred[4,1664]{1,0:T(4,128)(4,1)S(1)} %broadcast_compare_fusion.2, f32[4,1664,2,128]{1,3,2,0:T(8,128)} %copy.93, f32[1,4,128,2,128]{4,2,3,1,0:T(8,128)S(1)} %copy.94), kind=kOutput, calls=%fused_computation.3.clone.1 | convolution fusion | flops 2622356480 | bytes 14166528 | tf_op jit(solution)/shard_map/while/body/eval_jaxpr/gihe,gjhe->ghij/dot_general | solution.py:44
  305.7 10.2 %fusion.82 = f32[4,128,2,128]{1,3,2,0:T(8,128)S(1)} fusion(f32[4,1664,2,128]{1,3,2,0:T(8,128)} %copy.93, f32[4,2,128,1664]{3,2,1,0:T(8,128)S(1)} %get-tuple-element.197, f32[4,2,128]{2,1,0:T(2,128)S(1)} %get-tuple-element.198, pred[4,1664]{1,0:T(4,128)(4,1)S(1)} %broadcast_compare_fusion.2), kind=kOutput, calls=%fused_computation.10.clone.1 | convolution fusion | flops 2622357504 | bytes 14166528 | tf_op jit(solution)/shard_map/while/body/eval_jaxpr/ghij,gjhe->gihe/dot_general | solution.py:51
  317.4 14.2 %gather_fusion = f32[52,128,2,128]{3,2,1,0:T(2,128)} fusion(f32[64,128,2,128]{3,2,1,0:T(2,128)} %get-tuple-element.216, s32[1024]{0:T(1024)S(1)} %pad_clamp_fusion.2), kind=kCustom, calls=%fused_computation.clone.1 | custom fusion | bytes 13631696 | tf_op jit(solution)/shard_map/while/body/eval_jaxpr/gather | solution.py:42
  331.6 11.1 %copy.93 = f32[4,1664,2,128]{1,3,2,0:T(8,128)} copy(f32[4,1664,2,128]{3,2,1,0:T(2,128)} %bitcast.174) | data formatting | bytes 13631488 | tf_op jit(solution)/shard_map/while/body/eval_jaxpr/reshape | solution.py:43
  344.1 8.9 %fusion.81 = (f32[4,2,128]{2,1,0:T(2,128)S(1)}, f32[4,2,128,1664]{3,2,1,0:T(8,128)S(1)}) fusion(pred[4,1664]{1,0:T(4,128)(4,1)S(1)} %broadcast_compare_fusion.2, f32[4,1664,2,128]{1,3,2,0:T(8,128)} %copy.93, f32[1,4,128,2,128]{4,2,3,1,0:T(8,128)S(1)} %copy.94), kind=kOutput, calls=%fused_computation.3.clone.1 | convolution fusion | flops 2622356480 | bytes 14166528 | tf_op jit(solution)/shard_map/while/body/eval_jaxpr/gihe,gjhe->ghij/dot_general | solution.py:44
  354.5 10.2 %fusion.82 = f32[4,128,2,128]{1,3,2,0:T(8,128)S(1)} fusion(f32[4,1664,2,128]{1,3,2,0:T(8,128)} %copy.93, f32[4,2,128,1664]{3,2,1,0:T(8,128)S(1)} %get-tuple-element.197, f32[4,2,128]{2,1,0:T(2,128)S(1)} %get-tuple-element.198, pred[4,1664]{1,0:T(4,128)(4,1)S(1)} %broadcast_compare_fusion.2), kind=kOutput, calls=%fused_computation.10.clone.1 | convolution fusion | flops 2622357504 | bytes 14166528 | tf_op jit(solution)/shard_map/while/body/eval_jaxpr/ghij,gjhe->gihe/dot_general | solution.py:51
  366.2 14.2 %gather_fusion = f32[52,128,2,128]{3,2,1,0:T(2,128)} fusion(f32[64,128,2,128]{3,2,1,0:T(2,128)} %get-tuple-element.216, s32[1024]{0:T(1024)S(1)} %pad_clamp_fusion.2), kind=kCustom, calls=%fused_computation.clone.1 | custom fusion | bytes 13631696 | tf_op jit(solution)/shard_map/while/body/eval_jaxpr/gather | solution.py:42
  380.4 11.1 %copy.93 = f32[4,1664,2,128]{1,3,2,0:T(8,128)} copy(f32[4,1664,2,128]{3,2,1,0:T(2,128)} %bitcast.174) | data formatting | bytes 13631488 | tf_op jit(solution)/shard_map/while/body/eval_jaxpr/reshape | solution.py:43
  392.9 8.9 %fusion.81 = (f32[4,2,128]{2,1,0:T(2,128)S(1)}, f32[4,2,128,1664]{3,2,1,0:T(8,128)S(1)}) fusion(pred[4,1664]{1,0:T(4,128)(4,1)S(1)} %broadcast_compare_fusion.2, f32[4,1664,2,128]{1,3,2,0:T(8,128)} %copy.93, f32[1,4,128,2,128]{4,2,3,1,0:T(8,128)S(1)} %copy.94), kind=kOutput, calls=%fused_computation.3.clone.1 | convolution fusion | flops 2622356480 | bytes 14166528 | tf_op jit(solution)/shard_map/while/body/eval_jaxpr/gihe,gjhe->ghij/dot_general | solution.py:44
  403.3 10.2 %fusion.82 = f32[4,128,2,128]{1,3,2,0:T(8,128)S(1)} fusion(f32[4,1664,2,128]{1,3,2,0:T(8,128)} %copy.93, f32[4,2,128,1664]{3,2,1,0:T(8,128)S(1)} %get-tuple-element.197, f32[4,2,128]{2,1,0:T(2,128)S(1)} %get-tuple-element.198, pred[4,1664]{1,0:T(4,128)(4,1)S(1)} %broadcast_compare_fusion.2), kind=kOutput, calls=%fused_computation.10.clone.1 | convolution fusion | flops 2622357504 | bytes 14166528 | tf_op jit(solution)/shard_map/while/body/eval_jaxpr/ghij,gjhe->gihe/dot_general | solution.py:51
  415.0 14.2 %gather_fusion = f32[52,128,2,128]{3,2,1,0:T(2,128)} fusion(f32[64,128,2,128]{3,2,1,0:T(2,128)} %get-tuple-element.216, s32[1024]{0:T(1024)S(1)} %pad_clamp_fusion.2), kind=kCustom, calls=%fused_computation.clone.1 | custom fusion | bytes 13631696 | tf_op jit(solution)/shard_map/while/body/eval_jaxpr/gather | solution.py:42
  429.2 11.1 %copy.93 = f32[4,1664,2,128]{1,3,2,0:T(8,128)} copy(f32[4,1664,2,128]{3,2,1,0:T(2,128)} %bitcast.174) | data formatting | bytes 13631488 | tf_op jit(solution)/shard_map/while/body/eval_jaxpr/reshape | solution.py:43
  441.6 8.9 %fusion.81 = (f32[4,2,128]{2,1,0:T(2,128)S(1)}, f32[4,2,128,1664]{3,2,1,0:T(8,128)S(1)}) fusion(pred[4,1664]{1,0:T(4,128)(4,1)S(1)} %broadcast_compare_fusion.2, f32[4,1664,2,128]{1,3,2,0:T(8,128)} %copy.93, f32[1,4,128,2,128]{4,2,3,1,0:T(8,128)S(1)} %copy.94), kind=kOutput, calls=%fused_computation.3.clone.1 | convolution fusion | flops 2622356480 | bytes 14166528 | tf_op jit(solution)/shard_map/while/body/eval_jaxpr/gihe,gjhe->ghij/dot_general | solution.py:44
  452.0 10.2 %fusion.82 = f32[4,128,2,128]{1,3,2,0:T(8,128)S(1)} fusion(f32[4,1664,2,128]{1,3,2,0:T(8,128)} %copy.93, f32[4,2,128,1664]{3,2,1,0:T(8,128)S(1)} %get-tuple-element.197, f32[4,2,128]{2,1,0:T(2,128)S(1)} %get-tuple-element.198, pred[4,1664]{1,0:T(4,128)(4,1)S(1)} %broadcast_compare_fusion.2), kind=kOutput, calls=%fused_computation.10.clone.1 | convolution fusion | flops 2622357504 | bytes 14166528 | tf_op jit(solution)/shard_map/while/body/eval_jaxpr/ghij,gjhe->gihe/dot_general | solution.py:51
  463.1 2.5 copy.65
  465.7 5.4 all-to-all-start
  471.1 3.3 slice_bitcast_fusion
  474.4 22.4 %all-to-all-done = f32[2,8,128,128]{3,2,0,1:T(8,128)} async-done(((f32[2,8,128,128]{3,2,0,1:T(8,128)}), f32[2,8,128,128]{3,2,0,1:T(8,128)}, u32[]{:S(2)}, u32[]{:S(2)}) %all-to-all-start) | async-done | bytes 1048608 | tf_op jit(solution)/shard_map/all_to_all | solution.py:132
  498.7 6.2 %fusion.44 = (f32[256]{0:T(256)S(1)}, f32[256,1024]{1,0:T(8,128)S(1)}) fusion(f32[256,1024]{1,0:T(8,128)S(1)} %bitcast.187, f32[1024,1024]{1,0:T(8,128)} %param.14, f32[32,8,8,128]{3,2,1,0:T(8,128)S(1)} %bitcast.205), kind=kOutput, calls=%fused_computation.132 | convolution fusion | flops 3221749504 | bytes 7341056 | tf_op jit(solution)/shard_map/dot_general | solution.py:134
  506.3 2.7 broadcast_maximum_fusion
  509.0 4.5 max.34
  513.5 5.0 copy.69
  520.6 2.4 collective-permute-start.8
  523.1 2.5 copy.90
  525.6 4.1 max.37
  529.7 5.8 pad_maximum_fusion.2
  536.0 4.2 select_maximum_fusion
  540.2 10.9 %fusion.40 = (bf16[2,16,128,256]{3,0,2,1:T(2,128)(2,1)S(1)}, bf16[2,16,128,256]{3,0,2,1:T(2,128)(2,1)S(1)}, bf16[2,16,128,256]{3,0,2,1:T(2,128)(2,1)S(1)}, bf16[...) fusion(bf16[2,18,130,256]{3,0,2,1:T(2,128)(2,1)S(1)} %select_maxim, ...), kind=kLoop, calls=%fused_computation.128 | loop fusion | bytes 25165824 | tf_op jit(solution)/shard_map/slice | solution.py:69
  566.1 3.6 collective-permute-start.9
  569.8 6.4 %reshape.230 = f32[2,4,32,4,4,256]{5,4,3,2,1,0:T(4,128)} reshape(bf16[256,4096]{1,0:T(8,128)(2,1)} %get-tuple-element.157) | data formatting | bytes 6291456 | tf_op jit(solution)/shard_map/convert_element_type | solution.py:154
  576.2 5.3 copy.67
  581.5 5.4 reshape.229
  588.0 5.2 fusion.39
  602.9 2.2 add_convert_fusion
  (148 shorter events, 65.9 us)
Async XLA Ops:
  6.5 499.8 %copy-start = (bf16[256,4096]{1,0:T(8,128)(2,1)S(1)}, bf16[256,4096]{1,0:T(8,128)(2,1)}, u32[]{:S(2)}) copy-start(bf16[256,4096]{1,0:T(8,128)(2,1)} %param.17) | copy-start | bytes 6291460
  6.5 243.1 %all-gather.2.cloned.1.call-start = ((), (), s32[]{:S(2)}) async-start(), calls=%async_computation.1 | async-start | bytes 10485760 | tf_op jit(solution)/shard_map/all_gather | solution.py:115
  6.5 14.7 %collective-permute-start = (f32[2,128,1024]{2,1,0:T(8,128)}, f32[2,128,1024]{2,1,0:T(8,128)S(1)}, u32[]{:S(2)}, u32[]{:S(2)}) collective-permute-start(f32[2,128,1024]{2,1,0:T(8,128)} %param.12), channel_id=1, source_target_pairs={{0,1},{1,2},{2,3},{3,4},{4,5},{5,6},{6,7},{7,0},{8,9},{9,10},{10,1... | collective-permute-start | bytes 3145736 | tf_op jit(solution)/shard_map/ppermute | solution.py:19
  21.3 14.1 %collective-permute-start.1 = (f32[2,128,1024]{2,1,0:T(8,128)S(1)}, f32[2,128,1024]{2,1,0:T(8,128)S(1)}, u32[]{:S(2)}, u32[]{:S(2)}) collective-permute-start(f32[2,128,1024]{2,1,0:T(8,128)S(1)} %collective-permute-done), channel_id=1, source_target_pairs={{0,1},{1,2},{2,3},{3,4},{4,5},{5,6},{6,7},{7,0},{8,9},{9,10},{10,1... | collective-permute-start | bytes 3145736 | tf_op jit(solution)/shard_map/ppermute | solution.py:19
  35.4 1.0 copy-start.12
  36.4 14.2 %collective-permute-start.2 = (f32[2,128,1024]{2,1,0:T(8,128)S(1)}, f32[2,128,1024]{2,1,0:T(8,128)S(1)}, u32[]{:S(2)}, u32[]{:S(2)}) collective-permute-start(f32[2,128,1024]{2,1,0:T(8,128)S(1)} %collective-permute-done.1), channel_id=1, source_target_pairs={{0,1},{1,2},{2,3},{3,4},{4,5},{5,6},{6,7},{7,0},{8,9},{9,10},{10,1... | collective-permute-start | bytes 3145736 | tf_op jit(solution)/shard_map/ppermute | solution.py:19
  50.6 1.0 copy-start.14
  51.6 14.2 %collective-permute-start.3 = (f32[2,128,1024]{2,1,0:T(8,128)S(1)}, f32[2,128,1024]{2,1,0:T(8,128)S(1)}, u32[]{:S(2)}, u32[]{:S(2)}) collective-permute-start(f32[2,128,1024]{2,1,0:T(8,128)S(1)} %collective-permute-done.2), channel_id=1, source_target_pairs={{0,1},{1,2},{2,3},{3,4},{4,5},{5,6},{6,7},{7,0},{8,9},{9,10},{10,1... | collective-permute-start | bytes 3145736 | tf_op jit(solution)/shard_map/ppermute | solution.py:19
  65.8 1.0 copy-start.16
  66.8 14.2 %collective-permute-start.4 = (f32[2,128,1024]{2,1,0:T(8,128)S(1)}, f32[2,128,1024]{2,1,0:T(8,128)S(1)}, u32[]{:S(2)}, u32[]{:S(2)}) collective-permute-start(f32[2,128,1024]{2,1,0:T(8,128)S(1)} %collective-permute-done.3), channel_id=1, source_target_pairs={{0,1},{1,2},{2,3},{3,4},{4,5},{5,6},{6,7},{7,0},{8,9},{9,10},{10,1... | collective-permute-start | bytes 3145736 | tf_op jit(solution)/shard_map/ppermute | solution.py:19
  81.0 1.0 copy-start.18
  82.0 14.2 %collective-permute-start.5 = (f32[2,128,1024]{2,1,0:T(8,128)S(1)}, f32[2,128,1024]{2,1,0:T(8,128)}, u32[]{:S(2)}, u32[]{:S(2)}) collective-permute-start(f32[2,128,1024]{2,1,0:T(8,128)S(1)} %collective-permute-done.4), channel_id=1, source_target_pairs={{0,1},{1,2},{2,3},{3,4},{4,5},{5,6},{6,7},{7,0},{8,9},{9,10},{10,1... | collective-permute-start | bytes 3145736 | tf_op jit(solution)/shard_map/ppermute | solution.py:19
  96.2 14.6 %collective-permute-start.6 = (f32[2,128,1024]{2,1,0:T(8,128)}, f32[2,128,1024]{2,1,0:T(8,128)}, u32[]{:S(2)}, u32[]{:S(2)}) collective-permute-start(f32[2,128,1024]{2,1,0:T(8,128)} %collective-permute-done.5), channel_id=1, source_target_pairs={{0,1},{1,2},{2,3},{3,4},{4,5},{5,6},{6,7},{7,0},{8,9},{9,10},{10,1... | collective-permute-start | bytes 3145736 | tf_op jit(solution)/shard_map/ppermute | solution.py:19
  104.5 11.1 %copy-start.19 = (f32[2,128,1024]{2,1,0:T(8,128)S(1)}, f32[2,128,1024]{2,1,0:T(8,128)}, u32[]{:S(2)}) copy-start(f32[2,128,1024]{2,1,0:T(8,128)} %copy-done.18) | copy-start | bytes 3145732
  113.2 3.5 copy-start.17
  115.6 2.2 copy-start.15
  116.7 2.2 copy-start.13
  118.9 2.1 copy-start.6
  133.2 4.4 copy-start.9
  148.2 2.5 copy-start.23
  465.7 31.1 %all-to-all-start = ((f32[2,8,128,128]{3,2,0,1:T(8,128)}), f32[2,8,128,128]{3,2,0,1:T(8,128)}, u32[]{:S(2)}, u32[]{:S(2)}) async-start(f32[2,8,128,128]{3,2,0,1:T(8,128)} %copy.65), calls=%async_computation | async-start | bytes 2097152 | tf_op jit(solution)/shard_map/all_to_all | solution.py:132
  471.1 27.5 %copy-start.7 = (f32[2,128,1024]{2,1,0:T(8,128)S(1)}, f32[2,128,1024]{2,1,0:T(8,128)}, u32[]{:S(2)}) copy-start(f32[2,128,1024]{2,1,0:T(8,128)} %param.12) | copy-start | bytes 3145732
  498.7 6.5 %copy-start.20 = (f32[1024,256]{1,0:T(8,128)S(1)}, f32[1024,256]{1,0:T(8,128)}, u32[]{:S(2)}) copy-start(f32[1024,256]{1,0:T(8,128)} %param.16) | copy-start | bytes 3145732
  498.7 6.5 %copy-start.21 = (f32[1024]{0:T(1024)S(1)}, f32[1024]{0:T(1024)}, u32[]{:S(2)}) copy-start(f32[1024]{0:T(1024)} %param.15) | copy-start | bytes 12292
  513.5 9.5 %copy-start.22 = (f32[2,256]{1,0:T(2,128)S(1)}, f32[2,256]{1,0:T(2,128)}, u32[]{:S(2)}) copy-start(f32[2,256]{1,0:T(2,128)} %param.19) | copy-start | bytes 6148
  513.5 9.5 %copy-start.4 = (bf16[2,4,32,4,4,256]{5,4,3,2,1,0:T(4,128)(2,1)S(1)}, bf16[2,4,32,4,4,256]{5,4,3,2,1,0:T(4,128)(2,1)}, u32[]{:S(2)}) copy-start(bf16[2,4,32,4,4,256]{5,4,3,2,1,0:T(4,128)(2,1)} %max.34) | copy-start | bytes 6291460
  518.7 11.0 %collective-permute-start.7 = (bf16[2,1,128,256]{3,0,2,1:T(2,128)(2,1)S(1)}, bf16[2,1,128,256]{3,0,2,1:T(2,128)(2,1)S(1)}, u32[]{:S(2)}, u32[]{:S(2)}) collective-permute-start(bf16[2,1,128,256]{3,0,2,1:T(2,128)(2,1)S(1)} %get-tuple-element.150), channel_id=1, source_target_pairs={{0,1},{1,2},{2,3},{3,4},{4,5},{5,6},{6,7},{8,9},{9,10},{10,11},{11... | collective-permute-start | bytes 393224 | tf_op jit(solution)/shard_map/ppermute | solution.py:30
  520.6 9.1 %collective-permute-start.8 = (bf16[2,1,128,256]{3,0,2,1:T(2,128)(2,1)S(1)}, bf16[2,1,128,256]{3,0,2,1:T(2,128)(2,1)S(1)}, u32[]{:S(2)}, u32[]{:S(2)}) collective-permute-start(bf16[2,1,128,256]{3,0,2,1:T(2,128)(2,1)S(1)} %get-tuple-element.151), channel_id=1, source_target_pairs={{1,0},{2,1},{3,2},{4,3},{5,4},{6,5},{7,6},{9,8},{10,9},{11,10},{12... | collective-permute-start | bytes 393224 | tf_op jit(solution)/shard_map/ppermute | solution.py:33
  553.5 1.3 copy-start.11
  557.0 1.6 copy-start.8
  562.2 2.0 copy-start.2
  564.2 22.7 %collective-permute-start.10 = (bf16[2,1,128,256]{3,2,1,0:T(8,128)(2,1)S(1)}, bf16[2,1,128,256]{3,2,1,0:T(8,128)(2,1)S(1)}, u32[]{:S(2)}, u32[]{:S(2)}) collective-permute-start(bf16[2,1,128,256]{3,2,1,0:T(8,128)(2,1)S(1)} %get-tuple-element.147), channel_id=1, source_target_pairs={{1,0},{2,1},{3,2},{4,3},{5,4},{6,5},{7,6},{9,8},{10,9},{11,10},{12... | collective-permute-start | bytes 393224 | tf_op jit(solution)/shard_map/ppermute | solution.py:33
  566.1 20.8 %collective-permute-start.9 = (bf16[2,1,128,256]{3,2,1,0:T(8,128)(2,1)S(1)}, bf16[2,1,128,256]{3,2,1,0:T(8,128)(2,1)S(1)}, u32[]{:S(2)}, u32[]{:S(2)}) collective-permute-start(bf16[2,1,128,256]{3,2,1,0:T(8,128)(2,1)S(1)} %get-tuple-element.146), channel_id=1, source_target_pairs={{0,1},{1,2},{2,3},{3,4},{4,5},{5,6},{6,7},{8,9},{9,10},{10,11},{11... | collective-permute-start | bytes 393224 | tf_op jit(solution)/shard_map/ppermute | solution.py:30
  588.0 5.2 copy-start.10
  595.6 2.2 copy-start.3
  600.7 2.2 copy-start.5
  602.9 2.2 copy-start.1
Sparse Core Ops, SparseCore 0:
  150.8 98.7 all-gather.1
